TPU v7x, 32 devices: a whole 2x2x4 slice. The times are simulated.
32 devices in a mesh: ctx: 8 (over z, y), mp: 4 (over x, core).
Axes of the slice: x: 2, y: 2, z: 4, core: 2. Of those that a mesh axis runs over, the one named last changes fastest.
Arguments:
- q_in: bfloat16 [8192, 4096], P('ctx', 'mp'), may hold values from -6 to 6
- k_in: bfloat16 [8192, 4096], P('ctx', 'mp'), may hold values from -6 to 6
- v_in: bfloat16 [8192, 4096], P('ctx', 'mp'), may hold values from -6 to 6
- short_filter: float32 [3, 7, 4096], P(None, None, 'mp'), may hold values from -2 to 2
- taps: float32 [128, 4096], P(None, 'mp'), may hold values from -0.5 to 0.5
- residue: float32 [16, 4096], P(None, 'mp'), may hold values from -3 to 3
- rate: float32 [16, 4096], P(None, 'mp'), may hold values from 2.3692846e-06 to 0.033333335
- out_weight: bfloat16 [4096, 4096], P('mp', 'ctx'), may hold values from -0.09375 to 0.09375
Outputs:
- mixed: bfloat16 [8192, 4096], P('ctx', 'mp')
All inputs are finite; a program needn't handle non-finite values.
Results may differ from a plain program's by a relative error of at most 0.0095.
Values may be sent and summed in bfloat16 or wider, within the bound.
A program may use at most 192 MiB of HBM per device.

v0:
```python
import functools

import jax
import jax.numpy as jnp
import numpy as np
from jax import lax
from jax.experimental import pallas as pl
from jax.experimental.pallas import tpu as pltpu
from jax.sharding import PartitionSpec as P

SHORT_LEN = 7
LANES = 128
LEAD = 8


def shifted(array, axis):
    peers = lax.axis_size(axis)
    return lax.ppermute(array, axis, [(i, i + 1) for i in range(peers - 1)])


def split_const(matrix):
    high = matrix.astype(jnp.bfloat16)
    low = (matrix - high.astype(np.float64)).astype(jnp.bfloat16)
    return jnp.asarray(np.stack([high, low]))


@functools.lru_cache
def dft_matrices(block):
    size = 2 * block
    freq = np.arange(block)[:, None]
    pos = np.arange(block)[None, :]
    angle = 2 * np.pi * ((freq * pos) % size) / size
    fwd = np.concatenate([np.cos(angle), -np.sin(angle)])
    fwd[block] = 1.0 - 2.0 * (np.arange(block) % 2)
    out_pos = block + np.arange(block)[:, None]
    freq = np.arange(block)[None, :]
    angle = 2 * np.pi * ((freq * out_pos) % size) / size
    real = 2 * np.cos(angle)
    imag = -2 * np.sin(angle)
    real[:, 0] = 1.0
    imag[:, 0] = 1.0 - 2.0 * (np.arange(block) % 2)
    inv = np.concatenate([real, imag], 1) / size
    return fwd, fwd[:, ::-1], inv


def mm(a, b):
    return jnp.dot(a, b, preferred_element_type=jnp.float32)


def mm_wide(pair, values):
    high = values.astype(jnp.bfloat16)
    low = (values - high.astype(jnp.float32)).astype(jnp.bfloat16)
    return mm(pair[0], high) + mm(pair[0], low) + mm(pair[1], high)


def spectrum_parts(spec, block, row0):
    real, imag = spec[:block], spec[block:]
    return real, jnp.where(row0, 0.0, imag), jnp.where(row0, imag, real)


def spectrum_mul(parts, spec, block):
    real, imag, cross = parts
    sr, si = spec[:block], spec[block:]
    return real * sr - imag * si, cross * si + imag * sr


def fill(scratch, lead_rows, signal):
    scratch[:LEAD] = lead_rows.astype(jnp.float32)
    scratch[LEAD:] = signal.astype(jnp.float32)


def short_taps(scratch, filt, start, block):
    total = filt[0:1] * scratch[LEAD + start : LEAD + start + block]
    for lag in range(1, SHORT_LEN):
        first = LEAD + start - lag
        total = total + filt[lag : lag + 1] * scratch[first : first + block]
    return total


def local_kernel(
    k_ref, v_ref, lead_ref, filt_ref, taps_ref, res_ref, rate_ref, fwd_ref, rev_ref, inv_ref,
    y_ref, ends_ref, state_ref, tail_ref, ks, vs, gs,
):
    block = taps_ref.shape[0]
    pieces = k_ref.shape[0] // block
    modes = rate_ref.shape[0]
    fill(ks, lead_ref[1], k_ref[...])
    fill(vs, lead_ref[2], v_ref[...])
    for b in range(pieces):
        gated = short_taps(ks, filt_ref[1], b * block, block) * short_taps(
            vs, filt_ref[2], b * block, block
        )
        gs[b * block : (b + 1) * block] = gated.astype(jnp.bfloat16).astype(jnp.float32)
    rows = lax.broadcasted_iota(jnp.int32, (block, LANES), 0)
    back = (block - 1 - rows).astype(jnp.float32)

    def one_mode(n, h_rev):
        rate = rate_ref[pl.ds(n, 1), :]
        decay = jnp.exp(-rate * back)
        for b in range(pieces):
            ends_ref[n, b : b + 1, :] = jnp.sum(
                decay * gs[b * block : (b + 1) * block], axis=0, keepdims=True
            )
        return h_rev + (res_ref[pl.ds(n, 1), :] * jnp.sqrt(2.0 * rate)) * decay

    h_rev = lax.fori_loop(0, modes, one_mode, jnp.zeros((block, LANES), jnp.float32))

    step = jnp.exp(-rate_ref[...] * float(block))
    state = ends_ref[:, 0, :]
    for b in range(1, pieces):
        state = step * state + ends_ref[:, b, :]
    state_ref[...] = state

    row0 = rows == 0
    sign = (1 - 2 * (rows % 2)).astype(jnp.float32)
    sign = jnp.concatenate([sign, sign], 0)
    taps_spec = mm_wide(fwd_ref, taps_ref[...])
    near_spec = sign * (taps_spec + mm_wide(rev_ref, h_rev))
    far = spectrum_parts(taps_spec, block, row0)
    near = spectrum_parts(near_spec, block, row0)
    previous = None
    for b in range(pieces):
        signal = gs[b * block : (b + 1) * block].astype(jnp.bfloat16)
        spec = mm(fwd_ref[0], signal) + mm(fwd_ref[1], signal)
        real, imag = spectrum_mul(near, spec, block)
        if previous is not None:
            more_real, more_imag = spectrum_mul(far, previous, block)
            real, imag = real + more_real, imag + more_imag
        y_ref[b * block : (b + 1) * block] = mm_wide(inv_ref, jnp.concatenate([real, imag], 0))
        previous = spec
        if b == pieces - 1:
            tail_ref[...] = signal


def finish_kernel(
    y_ref, ends_ref, start_ref, tail_ref, q_ref, lead_ref, filt_ref, taps_ref, res_ref, rate_ref,
    fwd_ref, inv_ref, out_ref, qs, lift, states,
):
    block = taps_ref.shape[0]
    pieces = q_ref.shape[0] // block
    modes = rate_ref.shape[0]
    fill(qs, lead_ref[0], q_ref[...])
    rows = lax.broadcasted_iota(jnp.int32, (block, LANES), 0)
    ahead = (rows + 1).astype(jnp.float32)
    for n in range(modes):
        rate = rate_ref[n : n + 1, :]
        lift[n] = (res_ref[n : n + 1, :] * jnp.sqrt(2.0 * rate)) * jnp.exp(-rate * ahead)
    step = jnp.exp(-rate_ref[...] * float(block))
    state = start_ref[...]
    states[0] = state
    for b in range(1, pieces):
        state = step * state + ends_ref[:, b - 1, :]
        states[b] = state
    taps_spec = mm_wide(fwd_ref, taps_ref[...])
    far = spectrum_parts(taps_spec, block, rows == 0)
    tail = tail_ref[...]
    spec = mm(fwd_ref[0], tail) + mm(fwd_ref[1], tail)
    halo = mm_wide(inv_ref, jnp.concatenate(spectrum_mul(far, spec, block), 0))
    for b in range(pieces):
        span = slice(b * block, (b + 1) * block)
        total = y_ref[span]
        if b == 0:
            total = total + halo
        for n in range(modes):
            total = total + lift[n] * states[b, n : n + 1, :]
        q_short = short_taps(qs, filt_ref[0], b * block, block).astype(jnp.bfloat16)
        long_conv = total.astype(jnp.bfloat16)
        out_ref[span] = (q_short.astype(jnp.float32) * long_conv.astype(jnp.float32)).astype(
            jnp.bfloat16
        )


def cols(*lead):
    return pl.BlockSpec(lead + (LANES,), lambda i: (0,) * len(lead) + (i,))


def whole(shape):
    return pl.BlockSpec(shape, lambda i: (0,) * len(shape))


def local(q_in, k_in, v_in, short_filter, taps, residue, rate, out_weight):
    tokens, chans = q_in.shape
    block = taps.shape[0]
    modes = rate.shape[0]
    pieces = tokens // block
    fwd, rev, inv = [split_const(m) for m in dft_matrices(block)]
    grid = (chans // LANES,)
    f32, bf16 = jnp.float32, jnp.bfloat16
    lead = shifted(jnp.stack([q_in[-LEAD:], k_in[-LEAD:], v_in[-LEAD:]]), "ctx")
    filt_spec = cols(3, SHORT_LEN)
    params = pltpu.CompilerParams(vmem_limit_bytes=48 << 20)
    y_part, ends, state, tail = pl.pallas_call(
        local_kernel,
        grid=grid,
        in_specs=[
            cols(tokens), cols(tokens), cols(3, LEAD), filt_spec, cols(block), cols(modes),
            cols(modes), whole(fwd.shape), whole(rev.shape), whole(inv.shape),
        ],
        out_specs=[cols(tokens), cols(modes, pieces), cols(modes), cols(block)],
        out_shape=[
            jax.ShapeDtypeStruct((tokens, chans), f32),
            jax.ShapeDtypeStruct((modes, pieces, chans), f32),
            jax.ShapeDtypeStruct((modes, chans), f32),
            jax.ShapeDtypeStruct((block, chans), bf16),
        ],
        scratch_shapes=[
            pltpu.VMEM((LEAD + tokens, LANES), f32),
            pltpu.VMEM((LEAD + tokens, LANES), f32),
            pltpu.VMEM((tokens, LANES), f32),
        ],
        compiler_params=params,
        name="local_conv",
    )(k_in, v_in, lead, short_filter, taps, residue, rate, fwd, rev, inv)

    before = shifted(tail, "ctx")
    all_states = lax.all_gather(state, "ctx")
    gap = lax.axis_index("ctx") - 1 - jnp.arange(all_states.shape[0])
    spans = (jnp.maximum(gap, 0) * tokens).astype(f32)[:, None, None]
    carried = jnp.where((gap >= 0)[:, None, None], jnp.exp(-rate[None] * spans) * all_states, 0.0)
    start = jnp.sum(carried, axis=0)

    product = pl.pallas_call(
        finish_kernel,
        grid=grid,
        in_specs=[
            cols(tokens), cols(modes, pieces), cols(modes), cols(block), cols(tokens),
            cols(3, LEAD), filt_spec, cols(block), cols(modes), cols(modes),
            whole(fwd.shape), whole(inv.shape),
        ],
        out_specs=cols(tokens),
        out_shape=jax.ShapeDtypeStruct((tokens, chans), bf16),
        scratch_shapes=[
            pltpu.VMEM((LEAD + tokens, LANES), f32),
            pltpu.VMEM((modes, block, LANES), f32),
            pltpu.VMEM((pieces, modes, LANES), f32),
        ],
        compiler_params=params,
        name="finish_conv",
    )(y_part, ends, start, before, q_in, lead, short_filter, taps, residue, rate, fwd, inv)

    partial_sum = jnp.dot(
        product,
        lax.all_gather(out_weight, "ctx", axis=1, tiled=True),
        preferred_element_type=f32,
    )
    return lax.psum_scatter(partial_sum.astype(bf16), "mp", scatter_dimension=1, tiled=True)


def solution(mesh):
    in_specs = (
        P("ctx", "mp"),
        P("ctx", "mp"),
        P("ctx", "mp"),
        P(None, None, "mp"),
        P(None, "mp"),
        P(None, "mp"),
        P(None, "mp"),
        P("mp", "ctx"),
    )
    out_specs = P("ctx", "mp")
    return jax.shard_map(local, mesh=mesh, in_specs=in_specs, out_specs=out_specs, check_vma=False)
```

profile of v0, /device:TPU:7, one launch (start us, length us, event | category | flops | bytes accessed | tf_op | source)
XLA Modules:
  0.0 241.9 jit_solution(9221315783598006684)
XLA Ops:
  6.5 0.0 all-gather.3.cloned.1.call-start
  6.5 0.7 all-gather.3.cloned.1.call-update
  7.3 0.0 reduce-scatter.2.cloned.1.call-start
  7.3 0.7 slice_bitcast_fusion.2
  8.0 0.7 slice_bitcast_fusion
  8.8 3.1 %collective-permute-start = (bf16[3,8,1024]{2,1,0:T(8,128)(2,1)S(1)}, bf16[3,8,1024]{2,1,0:T(8,128)(2,1)S(1)}, u32[]{:S(2)}, u32[]{:S(2)}) collective-permute-start(bf16[3,8,1024]{2,1,0:T(8,128)(2,1)S(1)} %pad_maximum_fusion), channel_id=1, source_target_pairs={{0,4},{4,8},{8,12},{12,16},{16,20},{20,24},{24,28},{1,5},{5,9},{9,... | collective-permute-start | bytes 147464 | tf_op jit(solution)/shard_map/ppermute | solution.py:18
  12.0 0.8 neg.4
  12.8 0.0 copy-start
  12.8 0.8 collective-permute-done.lead_ref
  13.6 0.0 copy-start.1
  13.6 1.6 copy-done.1
  15.2 0.0 copy-start.2
  15.2 1.0 copy-done.2
  16.2 0.0 copy-start.3
  16.2 0.8 copy-done.3
  17.1 0.0 copy-start.4
  17.1 0.9 copy-done.4
  18.0 0.9 copy-done.5
  18.9 0.9 copy-done.6
  19.8 0.8 copy-done.7
  20.7 0.9 copy-done.8
  21.6 36.8 %local_conv.1 = (f32[1024,1024]{1,0:T(8,128)}, f32[16,8,1024]{2,1,0:T(8,128)S(1)}, f32[16,1024]{1,0:T(8,128)S(1)}, bf16[128,1024]{1,0:T(8,128)(2,1)S(1)}) custom-call(bf16[1024,1024]{1,0:T(8,128)(2,1)S(1)} %copy-done.1, bf16[1024,1024]{1,0:T(8,128)(2,1)} %v_ref.1, bf16[3,8,1024]{2,1,0:T(8,128)(2,1)S(1)} %collective-permute-done.lead_ref, ...), custom_call_target="tpu_custom_call" | custom-call | tf_op jit(solution)/shard_map/local_conv/pallas_call | solution.py:192
  58.4 4.0 %collective-permute-start.1 = (bf16[128,1024]{1,0:T(8,128)(2,1)S(1)}, bf16[128,1024]{1,0:T(8,128)(2,1)S(1)}, u32[]{:S(2)}, u32[]{:S(2)}) collective-permute-start(bf16[128,1024]{1,0:T(8,128)(2,1)S(1)} %get-tuple-element.12), channel_id=1, source_target_pairs={{0,4},{4,8},{8,12},{12,16},{16,20},{20,24},{24,28},{1,5},{5,9},{9,... | collective-permute-start | bytes 786440 | tf_op jit(solution)/shard_map/ppermute | solution.py:18
  62.4 55.1 %all-gather = f32[128,1024]{1,0:T(8,128)S(1)} all-gather(f32[16,1024]{1,0:T(8,128)S(1)} %get-tuple-element.11), channel_id=2, replica_groups=mesh['ctx'=8,'mp'=4] {'ctx'}, dimensions={0}, use_global_device_ids=true | all-gather | bytes 589824 | tf_op jit(solution)/shard_map/all_gather | solution.py:216
  117.6 0.2 select_reduce_fusion.start_ref
  117.7 0.0 collective-permute-done.1.tail_ref
  117.8 0.0 copy-done
  117.8 13.9 %finish_conv.1 = bf16[1024,1024]{1,0:T(8,128)(2,1)S(1)} custom-call(f32[1024,1024]{1,0:T(8,128)} %get-tuple-element.9.y_ref, f32[16,8,1024]{2,1,0:T(8,128)S(1)} %get-tuple-element.10.ends_ref, f32[16,1024]{1,0:T(8,128)S(1)} %select_reduce_fusion.start_ref, bf16[128,1024]{1,0:T(8,128)(2,1)S(1)} %collective-permute-done.1.tail_ref, ...), custom_call_target="tpu_custom_call" | custom-call | tf_op jit(solution)/shard_map/finish_conv/pallas_call | solution.py:222
  131.7 18.0 %all-gather.3.cloned.1.call-done = bf16[1024,4096]{1,0:T(8,128)(2,1)} async-done(((bf16[1024,512]{1,0:T(8,128)(2,1)}), bf16[1024,4096]{1,0:T(8,128)(2,1)}) %all-gather.3.cloned.1.call-update) | async-done | bytes 8388624 | tf_op jit(solution)/shard_map/all_gather | solution.py:243
  149.7 14.1 %convolution_convert_fusion = bf16[1024,4096]{1,0:T(8,128)(2,1)} fusion(bf16[1024,1024]{1,0:T(8,128)(2,1)S(1)} %finish_conv.1, bf16[1024,4096]{1,0:T(8,128)(2,1)} %all-gather.3.cloned.1.call-done), kind=kOutput, calls=%fused_computation | convolution fusion | flops 8594128896 | bytes 18874368 | tf_op jit(solution)/shard_map/dot_general | solution.py:241
  163.8 0.0 reduce-scatter.2.cloned.1.call-update
  163.8 71.2 %reduce-scatter.2.cloned.1.call-done = bf16[1024,1024]{1,0:T(8,128)(2,1)} async-done(((bf16[1024,4096]{1,0:T(8,128)(2,1)}), bf16[1024,1024]{1,0:T(8,128)(2,1)}) %reduce-scatter.2.cloned.1.call-update) | async-done | bytes 2097168 | tf_op jit(solution)/shard_map/reduce_scatter | solution.py:246
  (7 shorter events, 0.0 us)
Async XLA Ops:
  6.5 143.1 %all-gather.3.cloned.1.call-start = ((), (), s32[]{:S(2)}) async-start(), calls=%async_computation.1 | async-start | bytes 9437184 | tf_op jit(solution)/shard_map/all_gather | solution.py:243
  7.3 227.8 %reduce-scatter.2.cloned.1.call-start = ((), (), s32[]{:S(2)}) async-start(), calls=%async_computation.2 | async-start | bytes 10485760 | tf_op jit(solution)/shard_map/reduce_scatter | solution.py:246
  8.8 4.8 %collective-permute-start = (bf16[3,8,1024]{2,1,0:T(8,128)(2,1)S(1)}, bf16[3,8,1024]{2,1,0:T(8,128)(2,1)S(1)}, u32[]{:S(2)}, u32[]{:S(2)}) collective-permute-start(bf16[3,8,1024]{2,1,0:T(8,128)(2,1)S(1)} %pad_maximum_fusion), channel_id=1, source_target_pairs={{0,4},{4,8},{8,12},{12,16},{16,20},{20,24},{24,28},{1,5},{5,9},{9,... | collective-permute-start | bytes 147464 | tf_op jit(solution)/shard_map/ppermute | solution.py:18
  12.8 104.9 %copy-start = (bf16[1024,1024]{1,0:T(8,128)(2,1)S(1)}, bf16[1024,1024]{1,0:T(8,128)(2,1)}, u32[]{:S(2)}) copy-start(bf16[1024,1024]{1,0:T(8,128)(2,1)} %q_ref.1) | copy-start | bytes 6291460
  13.6 1.6 copy-start.1
  15.2 1.0 copy-start.2
  16.2 0.8 copy-start.3
  17.1 0.9 copy-start.4
  18.0 0.9 copy-start.5
  18.9 0.9 copy-start.6
  19.8 0.8 copy-start.7
  20.7 0.9 copy-start.8
  58.4 59.4 %collective-permute-start.1 = (bf16[128,1024]{1,0:T(8,128)(2,1)S(1)}, bf16[128,1024]{1,0:T(8,128)(2,1)S(1)}, u32[]{:S(2)}, u32[]{:S(2)}) collective-permute-start(bf16[128,1024]{1,0:T(8,128)(2,1)S(1)} %get-tuple-element.12), channel_id=1, source_target_pairs={{0,4},{4,8},{8,12},{12,16},{16,20},{20,24},{24,28},{1,5},{5,9},{9,... | collective-permute-start | bytes 786440 | tf_op jit(solution)/shard_map/ppermute | solution.py:18
Sparse Core Ops, SparseCore 0:
  9.4 140.2 all-gather.2
  164.0 71.0 reduce-scatter.1
where the time goes:
time: 245 us; the launch traced here: 242 us
  waiting for transfers between devices  90.7 us (37%)
  blocking collectives  55.1 us (22%)
  Pallas kernels  50.7 us (21%)
  matrix products  14.1 us (6%)
  between operations  13.5 us (6%)
  local copies, waits for them, and re-layouts  9.44 us (4%)
  starting transfers between devices  7.23 us (3%)
    reduce_scatter x1, waiting for transfers between devices, local(): lax.psum_scatter(partial_sum.astype(bf16), 'mp', scatter_dimension=1, til...  71.2 us
    all_gather x1, blocking collectives, local(): all_states = lax.all_gather(state, 'ctx')  55.1 us
    pallas_call x1, Pallas kernels, local(): pl.pallas_call(local_kernel, grid=grid, in_specs=[cols(tokens), cols(toke...  36.8 us
    all_gather x1, waiting for transfers between devices, local(): lax.all_gather(out_weight, 'ctx', axis=1, tiled=True)  18 us
    dot_general x1, matrix products, local(): jnp.dot(product, lax.all_gather(out_weight, 'ctx', axis=1, tiled=True), p...  14.1 us
    pallas_call x1, Pallas kernels, local(): pl.pallas_call(finish_kernel, grid=grid, in_specs=[cols(tokens), cols(mod...  13.9 us
    unnamed x18, local copies, waits for them, and re-layouts  7.98 us
    ppermute x2, starting transfers between devices, shifted(): return lax.ppermute(array, axis, [(i, i + 1) for i in range(peers - 1)])  7.19 us
  transfers between devices with their start and end apart: 4, of which 3 were waited for; matrix products, arithmetic and copies ran while one was open for 1% of the time, Pallas kernels for 21%

commit v1 on v0

--- a/solution.py
+++ b/solution.py
@@ -169,6 +169,191 @@
             jnp.bfloat16
         )
 
+MESH = pl.DeviceIdType.MESH
+
+
+def exchange_kernel(peers, state_ref, tail_ref, all_ref, before_ref, send, recv, tail_sems):
+    me = lax.axis_index("ctx")
+    barrier = pltpu.get_barrier_semaphore()
+    for hop in range(1, peers):
+        pl.semaphore_signal(
+            barrier, inc=1, device_id={"ctx": lax.rem(me + hop, peers)}, device_id_type=MESH
+        )
+    pl.semaphore_wait(barrier, peers - 1)
+
+    def tail_copy(peer):
+        return pltpu.make_async_remote_copy(
+            src_ref=tail_ref, dst_ref=before_ref, send_sem=tail_sems.at[0],
+            recv_sem=tail_sems.at[1], device_id={"ctx": peer}, device_id_type=MESH,
+        )
+
+    def state_copy(peer, slot, hop):
+        return pltpu.make_async_remote_copy(
+            src_ref=state_ref, dst_ref=all_ref.at[slot], send_sem=send.at[hop],
+            recv_sem=recv.at[slot], device_id={"ctx": peer}, device_id_type=MESH,
+        )
+
+    @pl.when(me < peers - 1)
+    def _():
+        tail_copy(me + 1).start()
+
+    for hop in range(1, peers):
+        state_copy(lax.rem(me + hop, peers), me, hop).start()
+    all_ref[me] = state_ref[...]
+
+    @pl.when(me == 0)
+    def _():
+        before_ref[...] = jnp.zeros_like(before_ref)
+
+    for hop in range(1, peers):
+        source = lax.rem(me + hop, peers)
+        state_copy(source, source, hop).wait_recv()
+        state_copy(source, me, hop).wait_send()
+
+    @pl.when(me > 0)
+    def _():
+        tail_copy(me).wait_recv()
+
+    @pl.when(me < peers - 1)
+    def _():
+        tail_copy(me + 1).wait_send()
+
+
+def exchange(state, tail):
+    peers = lax.axis_size("ctx")
+    vmem = pl.BlockSpec(memory_space=pltpu.VMEM)
+    return pl.pallas_call(
+        functools.partial(exchange_kernel, peers),
+        in_specs=[vmem] * 2,
+        out_specs=[vmem] * 2,
+        out_shape=[
+            jax.ShapeDtypeStruct((peers,) + state.shape, state.dtype),
+            jax.ShapeDtypeStruct(tail.shape, tail.dtype),
+        ],
+        scratch_shapes=[
+            pltpu.SemaphoreType.DMA((peers,)),
+            pltpu.SemaphoreType.DMA((peers,)),
+            pltpu.SemaphoreType.DMA((2,)),
+        ],
+        compiler_params=pltpu.CompilerParams(collective_id=0, has_side_effects=True),
+        name="state_exchange",
+    )(state, tail)
+
+
+def project_kernel(
+    prod_ref, w_ref, out_ref, near_out, near_in, far_out, far_in, mine_out, mine_in, hold, total,
+    sems,
+):
+    me = lax.axis_index("mp")
+    high, low = me // 2, lax.rem(me, 2)
+    pair = high * 2 + (1 - low)
+    across = (1 - high) * 2 + low
+    chunks, rows, width = near_out.shape
+    step = 256
+
+    barrier = pltpu.get_barrier_semaphore()
+    for peer in (pair, across):
+        pl.semaphore_signal(barrier, inc=1, device_id={"mp": peer}, device_id_type=MESH)
+    pl.semaphore_wait(barrier, 2)
+
+    def copy(kind, t, source, target, peer):
+        return pltpu.make_async_remote_copy(
+            src_ref=source.at[t], dst_ref=target.at[t], send_sem=sems.at[2 * kind, t],
+            recv_sem=sems.at[2 * kind + 1, t], device_id={"mp": peer}, device_id_type=MESH,
+        )
+
+    def near_copy(t):
+        return copy(0, t, near_out, near_in, pair)
+
+    def far_copy(t):
+        return copy(1, t, far_out, far_in, across)
+
+    def mine_copy(t):
+        return copy(2, t, mine_out, mine_in, pair)
+
+    def partial(t, owner, put):
+        left = prod_ref[pl.ds(pl.multiple_of(t * rows, rows), rows), :]
+        for col in range(0, width, step):
+            first = pl.multiple_of(owner * width + col, step)
+            put(col, mm(left, w_ref[:, pl.ds(first, step)]))
+
+    def send_near(t):
+        def put(col, value):
+            near_out[t, :, col : col + step] = value.astype(jnp.bfloat16)
+
+        partial(t, (1 - high) * 2 + (1 - low), put)
+        near_copy(t).start()
+
+        def keep(col, value):
+            hold[t, :, col : col + step] = value
+
+        partial(t, across, keep)
+
+    def send_far(t):
+        near_copy(t).wait_recv()
+        far_out[t] = (hold[t] + near_in[t].astype(jnp.float32)).astype(jnp.bfloat16)
+        far_copy(t).start()
+
+    def first_pass(t, carry):
+        send_near(t)
+
+        @pl.when(t > 0)
+        def _():
+            send_far(t - 1)
+
+        return carry
+
+    lax.fori_loop(0, chunks, first_pass, 0)
+    send_far(chunks - 1)
+
+    def second_pass(t, carry):
+        def put(col, value):
+            mine_out[t, :, col : col + step] = value.astype(jnp.bfloat16)
+
+        partial(t, pair, put)
+        mine_copy(t).start()
+
+        def keep(col, value):
+            total[t, :, col : col + step] = value
+
+        partial(t, me, keep)
+        return carry
+
+    lax.fori_loop(0, chunks, second_pass, 0)
+
+    def finish(t, carry):
+        mine_copy(t).wait_recv()
+        far_copy(t).wait_recv()
+        summed = total[t] + mine_in[t].astype(jnp.float32) + far_in[t].astype(jnp.float32)
+        out_ref[pl.ds(pl.multiple_of(t * rows, rows), rows), :] = summed.astype(jnp.bfloat16)
+        near_copy(t).wait_send()
+        far_copy(t).wait_send()
+        mine_copy(t).wait_send()
+        return carry
+
+    lax.fori_loop(0, chunks, finish, 0)
+
+
+def project(product, weight):
+    tokens = product.shape[0]
+    width = weight.shape[1] // lax.axis_size("mp")
+    chunks = 8
+    box = (chunks, tokens // chunks, width)
+    vmem = pl.BlockSpec(memory_space=pltpu.VMEM)
+    return pl.pallas_call(
+        project_kernel,
+        in_specs=[vmem] * 2,
+        out_specs=vmem,
+        out_shape=jax.ShapeDtypeStruct((tokens, width), jnp.bfloat16),
+        scratch_shapes=[pltpu.VMEM(box, jnp.bfloat16)] * 6
+        + [pltpu.VMEM(box, jnp.float32)] * 2
+        + [pltpu.SemaphoreType.DMA((6, chunks))],
+        compiler_params=pltpu.CompilerParams(
+            collective_id=1, has_side_effects=True, vmem_limit_bytes=48 << 20
+        ),
+        name="project",
+    )(product, weight)
+
 
 def cols(*lead):
     return pl.BlockSpec(lead + (LANES,), lambda i: (0,) * len(lead) + (i,))
@@ -212,8 +397,7 @@
         name="local_conv",
     )(k_in, v_in, lead, short_filter, taps, residue, rate, fwd, rev, inv)
 
-    before = shifted(tail, "ctx")
-    all_states = lax.all_gather(state, "ctx")
+    all_states, before = exchange(state, tail)
     gap = lax.axis_index("ctx") - 1 - jnp.arange(all_states.shape[0])
     spans = (jnp.maximum(gap, 0) * tokens).astype(f32)[:, None, None]
     carried = jnp.where((gap >= 0)[:, None, None], jnp.exp(-rate[None] * spans) * all_states, 0.0)
@@ -238,12 +422,7 @@
         name="finish_conv",
     )(y_part, ends, start, before, q_in, lead, short_filter, taps, residue, rate, fwd, inv)
 
-    partial_sum = jnp.dot(
-        product,
-        lax.all_gather(out_weight, "ctx", axis=1, tiled=True),
-        preferred_element_type=f32,
-    )
-    return lax.psum_scatter(partial_sum.astype(bf16), "mp", scatter_dimension=1, tiled=True)
+    return project(product, lax.all_gather(out_weight, "ctx", axis=1, tiled=True))
 
 
 def solution(mesh):

time: 245 us -> 216 us (0.88)
  Pallas kernels: 50.7 us -> 138 us
  blocking collectives: 55.1 us -> 0 us
  waiting for transfers between devices: 90.7 us -> 41.2 us
  matrix products: 14.1 us -> 0 us
  local copies, waits for them, and re-layouts: 9.44 us -> 16.3 us
  starting transfers between devices: 7.23 us -> 3.15 us
    pallas_call x0 -> x2, Pallas kernels: none -> 87.4 us  [the longest x1 53.3 us: project(): pl.pallas_call(project_kernel, in_specs=[vmem] * 2, out_specs=vmem, out_s...]
    reduce_scatter x1 -> x0, waiting for transfers between devices: 71.2 us -> none  [local(): lax.psum_scatter(partial_sum.astype(bf16), 'mp', scatter_dimension=1, til...]
    all_gather x1 -> x0, blocking collectives: 55.1 us -> none  [local(): all_states = lax.all_gather(state, 'ctx')]
    all_gather x1, waiting for transfers between devices: 18 us -> 39.6 us  [local(): lax.all_gather(out_weight, 'ctx', axis=1, tiled=True)]
    dot_general x1 -> x0, matrix products: 14.1 us -> none  [local(): jnp.dot(product, lax.all_gather(out_weight, 'ctx', axis=1, tiled=True), p...]
    unnamed x18 -> x41, local copies, waits for them, and re-layouts: 7.98 us -> 14.9 us
    ppermute x2 -> x1, starting transfers between devices: 7.19 us -> 3.15 us  [shifted(): return lax.ppermute(array, axis, [(i, i + 1) for i in range(peers - 1)])]
  transfers between devices with their start and end apart: 4 -> 2, of which waited for: 3 -> 2; matrix products, arithmetic and copies ran while one was open for 1% -> 2% of each run, Pallas kernels for 21% -> 40%
where the time goes in v1:
time: 216 us; the launch traced here: 214 us
  Pallas kernels  138 us (64%)
  waiting for transfers between devices  41.2 us (19%)
  local copies, waits for them, and re-layouts  16.3 us (8%)
  between operations  13.5 us (6%)
  starting transfers between devices  3.15 us (1%)
    pallas_call x1, Pallas kernels, project(): pl.pallas_call(project_kernel, in_specs=[vmem] * 2, out_specs=vmem, out_s...  53.3 us
    all_gather x1, waiting for transfers between devices, local(): lax.all_gather(out_weight, 'ctx', axis=1, tiled=True)  39.6 us
    pallas_call x1, Pallas kernels, local(): pl.pallas_call(local_kernel, grid=grid, in_specs=[cols(tokens), cols(toke...  36.9 us
    pallas_call x1, Pallas kernels, exchange(): pl.pallas_call(functools.partial(exchange_kernel, peers), in_specs=[vmem]...  34 us
    unnamed x41, local copies, waits for them, and re-layouts  14.9 us
    pallas_call x1, Pallas kernels, local(): pl.pallas_call(finish_kernel, grid=grid, in_specs=[cols(tokens), cols(mod...  13.9 us
  transfers between devices with their start and end apart: 2, of which 2 were waited for; matrix products, arithmetic and copies ran while one was open for 2% of the time, Pallas kernels for 40%

profile of v1, /device:TPU:7, one launch (start us, length us, event | category | flops | bytes accessed | tf_op | source)
XLA Modules:
  0.0 214.5 jit_solution(12298721409525553790)
XLA Ops:
  6.5 0.0 all-gather.2.cloned.1.call-start
  6.5 0.7 all-gather.2.cloned.1.call-update
  7.3 0.7 slice_bitcast_fusion.2
  8.0 0.7 slice_bitcast_fusion
  8.7 3.1 %collective-permute-start = (bf16[3,8,1024]{2,1,0:T(8,128)(2,1)S(1)}, bf16[3,8,1024]{2,1,0:T(8,128)(2,1)S(1)}, u32[]{:S(2)}, u32[]{:S(2)}) collective-permute-start(bf16[3,8,1024]{2,1,0:T(8,128)(2,1)S(1)} %pad_maximum_fusion), channel_id=1, source_target_pairs={{0,4},{4,8},{8,12},{12,16},{16,20},{20,24},{24,28},{1,5},{5,9},{9,... | collective-permute-start | bytes 147464 | tf_op jit(solution)/shard_map/ppermute | solution.py:18
  11.9 0.8 neg.4
  12.8 0.8 collective-permute-done.lead_ref
  13.6 1.6 copy-done.1
  15.2 1.0 copy-done.2
  16.2 0.8 copy-done.4
  17.0 0.9 copy-done.6
  17.9 0.9 copy-done.8
  18.9 0.9 copy-done.10
  19.8 0.8 copy-done.12
  20.6 0.9 copy-done.18
  21.6 0.0 copy-start.9
  21.6 0.0 copy-start.13
  21.6 36.9 %local_conv.1 = (f32[1024,1024]{1,0:T(8,128)}, f32[16,8,1024]{2,1,0:T(8,128)S(1)}, f32[16,1024]{1,0:T(8,128)S(1)}, bf16[128,1024]{1,0:T(8,128)(2,1)S(1)}) custom-call(bf16[1024,1024]{1,0:T(8,128)(2,1)S(1)} %copy-done.1, bf16[1024,1024]{1,0:T(8,128)(2,1)} %v_ref.1, bf16[3,8,1024]{2,1,0:T(8,128)(2,1)S(1)} %collective-permute-done.lead_ref, ...), custom_call_target="tpu_custom_call" | custom-call | tf_op jit(solution)/shard_map/local_conv/pallas_call | solution.py:377
  58.5 0.0 copy-done.16
  58.5 0.7 copy-done.15
  59.2 0.6 copy-done.19
  59.8 34.0 %state_exchange.1 = (f32[8,16,1024]{2,1,0:T(8,128)}, bf16[128,1024]{1,0:T(8,128)(2,1)}) custom-call(f32[16,1024]{1,0:T(8,128)} %copy-done.19, bf16[128,1024]{1,0:T(8,128)(2,1)} %copy-done.15), custom_call_target="tpu_custom_call" | custom-call | tf_op jit(solution)/shard_map/state_exchange/pallas_call | solution.py:225
  93.9 1.2 select_reduce_fusion.start_ref
  95.2 0.0 copy-start
  95.2 1.6 copy-done
  96.8 0.9 copy-done.11
  97.7 0.9 copy-done.14
  98.6 0.8 copy-done.17
  99.4 13.9 %finish_conv.1.prod_ref = bf16[1024,1024]{1,0:T(8,128)(2,1)S(1)} custom-call(f32[1024,1024]{1,0:T(8,128)} %get-tuple-element.11.y_ref, f32[16,8,1024]{2,1,0:T(8,128)S(1)} %get-tuple-element.12.ends_ref, f32[16,1024]{1,0:T(8,128)S(1)} %select_reduce_fusion.start_ref, bf16[128,1024]{1,0:T(8,128)(2,1)S(1)} %copy-done.14, bf16[1024,1024]{1,0:T(8,128)(2,1)S(1)} %copy-done, ...), custom_call_target="tpu_custom_call" | custom-call | tf_op jit(solution)/shard_map/finish_conv/pallas_call | solution.py:406
  113.3 39.6 %all-gather.2.cloned.1.call-done.w_ref = bf16[1024,4096]{1,0:T(8,128)(2,1)} async-done(((bf16[1024,512]{1,0:T(8,128)(2,1)}), bf16[1024,4096]{1,0:T(8,128)(2,1)}) %all-gather.2.cloned.1.call-update) | async-done | bytes 8388624 | tf_op jit(solution)/shard_map/all_gather | solution.py:425
  153.0 53.3 %project.1 = bf16[1024,1024]{1,0:T(8,128)(2,1)S(1)} custom-call(bf16[1024,1024]{1,0:T(8,128)(2,1)S(1)} %finish_conv.1.prod_ref, bf16[1024,4096]{1,0:T(8,128)(2,1)} %all-gather.2.cloned.1.call-done.w_ref), custom_call_target="tpu_custom_call" | custom-call | tf_op jit(solution)/shard_map/project/pallas_call | solution.py:343
  206.3 1.3 copy.13
  (25 shorter events, 0.1 us)
Async XLA Ops:
  6.5 146.4 %all-gather.2.cloned.1.call-start = ((), (), s32[]{:S(2)}) async-start(), calls=%async_computation | async-start | bytes 9437184 | tf_op jit(solution)/shard_map/all_gather | solution.py:425
  8.7 4.8 %collective-permute-start = (bf16[3,8,1024]{2,1,0:T(8,128)(2,1)S(1)}, bf16[3,8,1024]{2,1,0:T(8,128)(2,1)S(1)}, u32[]{:S(2)}, u32[]{:S(2)}) collective-permute-start(bf16[3,8,1024]{2,1,0:T(8,128)(2,1)S(1)} %pad_maximum_fusion), channel_id=1, source_target_pairs={{0,4},{4,8},{8,12},{12,16},{16,20},{20,24},{24,28},{1,5},{5,9},{9,... | collective-permute-start | bytes 147464 | tf_op jit(solution)/shard_map/ppermute | solution.py:18
  13.6 1.6 copy-start.1
  15.2 1.0 copy-start.2
  16.2 0.8 copy-start.4
  17.0 0.9 copy-start.6
  17.9 0.9 copy-start.8
  18.9 0.9 copy-start.10
  19.8 0.8 copy-start.12
  20.6 0.9 copy-start.18
  21.5 37.0 %copy-start.16 = (bf16[3,8,1024]{2,1,0:T(8,128)(2,1)}, bf16[3,8,1024]{2,1,0:T(8,128)(2,1)S(1)}, u32[]{:S(2)}) copy-start(bf16[3,8,1024]{2,1,0:T(8,128)(2,1)S(1)} %collective-permute-done.lead_ref) | copy-start | bytes 147460
  21.5 73.6 %copy-start.3 = (f32[128,1024]{1,0:T(8,128)S(1)}, f32[128,1024]{1,0:T(8,128)}, u32[]{:S(2)}) copy-start(f32[128,1024]{1,0:T(8,128)} %taps_ref.3) | copy-start | bytes 1572868
  21.6 73.6 %copy-start.5 = (f32[16,1024]{1,0:T(8,128)S(1)}, f32[16,1024]{1,0:T(8,128)}, u32[]{:S(2)}) copy-start(f32[16,1024]{1,0:T(8,128)} %rate_ref.3) | copy-start | bytes 196612
  21.6 73.6 %copy-start.7 = (bf16[2,256,128]{2,1,0:T(8,128)(2,1)S(1)}, bf16[2,256,128]{2,1,0:T(8,128)(2,1)}, u32[]{:S(2)}) copy-start(bf16[2,256,128]{2,1,0:T(8,128)(2,1)} %constant.21.clone.fwd_ref) | copy-start | bytes 393220
  21.6 73.6 %copy-start.9 = (bf16[2,128,256]{2,1,0:T(8,128)(2,1)S(1)}, bf16[2,128,256]{2,1,0:T(8,128)(2,1)}, u32[]{:S(2)}) copy-start(bf16[2,128,256]{2,1,0:T(8,128)(2,1)} %constant.23.clone.inv_ref) | copy-start | bytes 393220
  21.6 73.6 %copy-start.13 = (f32[16,1024]{1,0:T(8,128)S(1)}, f32[16,1024]{1,0:T(8,128)}, u32[]{:S(2)}) copy-start(f32[16,1024]{1,0:T(8,128)} %res_ref.3) | copy-start | bytes 196612
  58.5 0.7 copy-start.15
  59.2 0.6 copy-start.19
  95.2 1.6 copy-start
  96.8 0.9 copy-start.11
  97.7 0.9 copy-start.14
  98.6 0.8 copy-start.17
Sparse Core Ops, SparseCore 0:
  9.4 143.5 all-gather.1

commit v2 on v1

--- a/solution.py
+++ b/solution.py
@@ -355,6 +355,247 @@
     )(product, weight)
 
 
+def ring_place(chip, count):
+    odd = chip % 2
+    return (chip // 2) * (1 - odd) + (count - 1 - chip // 2) * odd
+
+
+def ring_chip(place, count):
+    back = place // (count // 2)
+    return 2 * place * (1 - back) + (2 * (count - 1 - place) + 1) * back
+
+
+def ring_project_kernel(
+    peers, prod_ref, w_ref, own_ref, out_ref, near_out, near_in, far_out, far_in, mine_out,
+    mine_in, hold, total, ring, pair_out, pair_in, cross_out, cross_in, kept, sems, ring_sems,
+    unit_sems,
+):
+    me = lax.axis_index("mp")
+    high, low = me // 2, lax.rem(me, 2)
+    pair = high * 2 + (1 - low)
+    across = (1 - high) * 2 + low
+    place = ring_place(lax.axis_index("ctx"), peers)
+    chunks, rows, width = near_out.shape
+    step = own_ref.shape[1]
+    row_step = 256
+
+    def neighbour(offset):
+        return lax.rem(place + offset + peers, peers)
+
+    ahead, behind = ring_chip(neighbour(1), peers), ring_chip(neighbour(-1), peers)
+    barrier = pltpu.get_barrier_semaphore()
+    for peer in (pair, across):
+        pl.semaphore_signal(barrier, inc=1, device_id={"mp": peer}, device_id_type=MESH)
+    for peer in (ahead, behind):
+        pl.semaphore_signal(barrier, inc=1, device_id={"ctx": peer}, device_id_type=MESH)
+    pl.semaphore_wait(barrier, 4)
+
+    def ring_copy(way, hop, first):
+        owner = ring_chip(neighbour(-hop if way == 0 else hop), peers)
+        return pltpu.make_async_remote_copy(
+            src_ref=own_ref if first else ring.at[owner], dst_ref=ring.at[owner],
+            send_sem=ring_sems.at[2 * way, hop], recv_sem=ring_sems.at[2 * way + 1, hop],
+            device_id={"ctx": behind if way else ahead}, device_id_type=MESH,
+        )
+
+    hops = (peers // 2, peers - 1 - peers // 2)
+    for way in (0, 1):
+        ring_copy(way, 0, True).start()
+
+    def copy(kind, t, source, target, peer):
+        return pltpu.make_async_remote_copy(
+            src_ref=source.at[t], dst_ref=target.at[t], send_sem=sems.at[2 * kind, t],
+            recv_sem=sems.at[2 * kind + 1, t], device_id={"mp": peer}, device_id_type=MESH,
+        )
+
+    def near_copy(t):
+        return copy(0, t, near_out, near_in, pair)
+
+    def far_copy(t):
+        return copy(1, t, far_out, far_in, across)
+
+    def mine_copy(t):
+        return copy(2, t, mine_out, mine_in, pair)
+
+    def partial(t, owner, put):
+        left = prod_ref[pl.ds(pl.multiple_of(t * rows, rows), rows), :]
+        for col in range(0, width, step):
+            first = pl.multiple_of(owner * width + col, step)
+            put(col, mm(left, w_ref[:, pl.ds(first, step)]))
+
+    def send_far(t):
+        near_copy(t).wait_recv()
+        far_out[t] = (hold[t] + near_in[t].astype(jnp.float32)).astype(jnp.bfloat16)
+        far_copy(t).start()
+
+    def first_pass(t, carry):
+        def put(col, value):
+            near_out[t, :, col : col + step] = value.astype(jnp.bfloat16)
+
+        partial(t, (1 - high) * 2 + (1 - low), put)
+        near_copy(t).start()
+
+        def keep(col, value):
+            hold[t, :, col : col + step] = value
+
+        partial(t, across, keep)
+
+        @pl.when(t > 0)
+        def _():
+            send_far(t - 1)
+
+        return carry
+
+    lax.fori_loop(0, chunks, first_pass, 0)
+    send_far(chunks - 1)
+
+    def second_pass(t, carry):
+        def put(col, value):
+            mine_out[t, :, col : col + step] = value.astype(jnp.bfloat16)
+
+        partial(t, pair, put)
+        mine_copy(t).start()
+
+        def keep(col, value):
+            total[t, :, col : col + step] = value
+
+        partial(t, me, keep)
+        return carry
+
+    lax.fori_loop(0, chunks, second_pass, 0)
+
+    def pair_copy(slot):
+        return pltpu.make_async_remote_copy(
+            src_ref=pair_out.at[slot], dst_ref=pair_in.at[slot], send_sem=unit_sems.at[0, slot],
+            recv_sem=unit_sems.at[1, slot], device_id={"mp": pair}, device_id_type=MESH,
+        )
+
+    def cross_copy(slot):
+        return pltpu.make_async_remote_copy(
+            src_ref=cross_out.at[slot], dst_ref=cross_in.at[slot],
+            send_sem=unit_sems.at[2, slot], recv_sem=unit_sems.at[3, slot],
+            device_id={"mp": across}, device_id_type=MESH,
+        )
+
+    def unit(chip, first):
+        owner, sub = chip // 2, lax.rem(chip, 2)
+        gap = owner // 2 - high
+        same = 1 - gap * gap
+        slot = same * 2 + sub
+        mine = lax.rem(owner, 2) == low
+
+        def products(put):
+            def body(r, carry):
+                at = pl.ds(pl.multiple_of(r * row_step, row_step), row_step)
+                right = own_ref[...] if first else ring[chip]
+                put(at, mm(prod_ref[at, :], right))
+                return carry
+
+            lax.fori_loop(0, prod_ref.shape[0] // row_step, body, 0)
+
+        @pl.when(jnp.logical_not(mine))
+        def _():
+            def put(at, value):
+                pair_out[slot, at, :] = value.astype(jnp.bfloat16)
+
+            products(put)
+            pair_copy(slot).start()
+
+        @pl.when(mine)
+        def _():
+            def put(at, value):
+                kept[slot, at, :] = value
+
+            products(put)
+
+            @pl.when(same == 0)
+            def _():
+                pair_copy(slot).wait_recv()
+                cross_out[sub] = (kept[slot] + pair_in[slot].astype(jnp.float32)).astype(
+                    jnp.bfloat16
+                )
+                cross_copy(sub).start()
+
+    unit(ring_chip(place, peers), True)
+
+    def arrived(way, hop):
+        return ring_chip(neighbour(-hop - 1 if way == 0 else hop + 1), peers)
+
+    for hop in range(hops[0]):
+        ways = [way for way in (0, 1) if hop < hops[way]]
+        for way in ways:
+            pltpu.make_async_remote_copy(
+                src_ref=own_ref, dst_ref=ring.at[arrived(way, hop)],
+                send_sem=ring_sems.at[2 * way, hop], recv_sem=ring_sems.at[2 * way + 1, hop],
+                device_id={"ctx": behind if way else ahead}, device_id_type=MESH,
+            ).wait_recv()
+            if hop + 1 < hops[way]:
+                ring_copy(way, hop + 1, False).start()
+        for way in ways:
+            unit(arrived(way, hop), False)
+
+    def finish(t, carry):
+        mine_copy(t).wait_recv()
+        far_copy(t).wait_recv()
+        summed = total[t] + mine_in[t].astype(jnp.float32) + far_in[t].astype(jnp.float32)
+        at = pl.ds(pl.multiple_of(t * rows, rows), rows)
+        for part in range(width // step):
+            out_ref[at, 2 * part * step : (2 * part + 1) * step] = summed[
+                :, part * step : (part + 1) * step
+            ].astype(jnp.bfloat16)
+        near_copy(t).wait_send()
+        far_copy(t).wait_send()
+        mine_copy(t).wait_send()
+        return carry
+
+    lax.fori_loop(0, chunks, finish, 0)
+    for sub in range(2):
+        pair_copy(2 + sub).wait_recv()
+        cross_copy(sub).wait_recv()
+        summed = kept[2 + sub] + pair_in[2 + sub].astype(jnp.float32)
+        out_ref[:, (2 * sub + 1) * step : (2 * sub + 2) * step] = (
+            summed + cross_in[sub].astype(jnp.float32)
+        ).astype(jnp.bfloat16)
+        pair_copy(sub).wait_send()
+        pair_copy(2 + sub).wait_send()
+        cross_copy(sub).wait_send()
+    for way in (0, 1):
+        for hop in range(hops[way]):
+            ring_copy(way, hop, hop == 0).wait_send()
+
+
+def ring_project(product, weight, own):
+    tokens = product.shape[0]
+    peers = lax.axis_size("ctx")
+    step = own.shape[1]
+    width = weight.shape[1] // lax.axis_size("mp")
+    chunks = 4
+    box = (chunks, tokens // chunks, width)
+    bf16, f32 = jnp.bfloat16, jnp.float32
+    vmem = pl.BlockSpec(memory_space=pltpu.VMEM)
+    return pl.pallas_call(
+        functools.partial(ring_project_kernel, peers),
+        in_specs=[vmem] * 3,
+        out_specs=vmem,
+        out_shape=jax.ShapeDtypeStruct((tokens, 2 * width), bf16),
+        scratch_shapes=[pltpu.VMEM(box, bf16)] * 6
+        + [pltpu.VMEM(box, f32)] * 2
+        + [pltpu.VMEM((peers,) + own.shape, bf16)]
+        + [pltpu.VMEM((4, tokens, step), bf16)] * 2
+        + [pltpu.VMEM((2, tokens, step), bf16)] * 2
+        + [pltpu.VMEM((4, tokens, step), f32)]
+        + [
+            pltpu.SemaphoreType.DMA((6, chunks)),
+            pltpu.SemaphoreType.DMA((4, peers)),
+            pltpu.SemaphoreType.DMA((4, 4)),
+        ],
+        compiler_params=pltpu.CompilerParams(
+            collective_id=2, has_side_effects=True, vmem_limit_bytes=52 << 20
+        ),
+        name="ring_project",
+    )(product, weight, own)
+
+
 def cols(*lead):
     return pl.BlockSpec(lead + (LANES,), lambda i: (0,) * len(lead) + (i,))
 
@@ -422,6 +663,12 @@
         name="finish_conv",
     )(y_part, ends, start, before, q_in, lead, short_filter, taps, residue, rate, fwd, inv)
 
+    columns = out_weight.shape[1]
+    peers, groups = lax.axis_size("ctx"), lax.axis_size("mp")
+    if peers == 2 * groups and columns % 256 == 0:
+        half = columns // 2
+        early = lax.all_gather(out_weight[:, :half], "ctx", axis=1, tiled=True)
+        return ring_project(product, early, out_weight[:, half:])
     return project(product, lax.all_gather(out_weight, "ctx", axis=1, tiled=True))
 
 

time: 216 us -> 198 us (0.917)
  waiting for transfers between devices: 41.2 us -> 1.23 us
  Pallas kernels: 138 us -> 158 us
  local copies, waits for them, and re-layouts: 16.3 us -> 18.9 us
    all_gather x1, waiting for transfers between devices: 39.6 us -> 0.01 us  [local(): early = lax.all_gather(out_weight[:, :half], 'ctx', axis=1, tiled=True)]
    pallas_call x1, Pallas kernels: 53.3 us -> 78.5 us  [ring_project(): pl.pallas_call(functools.partial(ring_project_kernel, peers), in_specs=[v...]
    pallas_call x1, Pallas kernels: 34 us -> 29.2 us  [exchange(): pl.pallas_call(functools.partial(exchange_kernel, peers), in_specs=[vmem]...]
    slice x0 -> x1, local copies, waits for them, and re-layouts: none -> 2.28 us  [local(): return ring_project(product, early, out_weight[:, half:])]
  transfers between devices with their start and end apart: 2 -> 2, of which waited for: 2 -> 1; matrix products, arithmetic and copies ran while one was open for 2% -> 2% of each run, Pallas kernels for 40% -> 40%
where the time goes in v2:
time: 198 us
  Pallas kernels  158 us (80%)
  local copies, waits for them, and re-layouts  18.9 us (10%)
  between operations  13.5 us (7%)
  starting transfers between devices  3.17 us (2%)
  other arithmetic  2.51 us (1%)
    pallas_call x1, Pallas kernels, ring_project(): pl.pallas_call(functools.partial(ring_project_kernel, peers), in_specs=[v...  78.5 us
    pallas_call x1, Pallas kernels, local(): pl.pallas_call(local_kernel, grid=grid, in_specs=[cols(tokens), cols(toke...  36.8 us
    pallas_call x1, Pallas kernels, exchange(): pl.pallas_call(functools.partial(exchange_kernel, peers), in_specs=[vmem]...  29.2 us
    unnamed x41, local copies, waits for them, and re-layouts  15.9 us
    pallas_call x1, Pallas kernels, local(): pl.pallas_call(finish_kernel, grid=grid, in_specs=[cols(tokens), cols(mod...  13.9 us
  transfers between devices with their start and end apart: 2, of which 1 were waited for; matrix products, arithmetic and copies ran while one was open for 2% of the time, Pallas kernels for 40%

profile of v2, /device:TPU:7, one launch (start us, length us, event | category | flops | bytes accessed | tf_op | source)
XLA Modules:
  0.0 197.7 jit_solution(1475186613186601012)
XLA Ops:
  6.5 0.0 all-gather.2.cloned.1.call-start
  6.6 2.3 %fusion.1 = (bf16[1024,256]{1,0:T(8,128)(2,1)S(1)}, bf16[1024,256]{1,0:T(8,128)(2,1)}) fusion(bf16[1024,512]{1,0:T(8,128)(2,1)} %param.18), kind=kLoop, calls=%fused_computation.8 | loop fusion | bytes 2097152 | tf_op jit(solution)/shard_map/slice | solution.py:671
  8.9 0.0 all-gather.2.cloned.1.call-update
  8.9 0.0 copy-done.1
  8.9 0.7 slice_bitcast_fusion
  9.7 0.6 pad_maximum_fusion
  10.3 3.1 %collective-permute-start = (bf16[3,8,1024]{2,1,0:T(8,128)(2,1)}, bf16[3,8,1024]{2,1,0:T(8,128)(2,1)S(1)}, u32[]{:S(2)}, u32[]{:S(2)}) collective-permute-start(bf16[3,8,1024]{2,1,0:T(8,128)(2,1)} %pad_maximum_fusion), channel_id=1, source_target_pairs={{0,4},{4,8},{8,12},{12,16},{16,20},{20,24},{24,28},{1,5},{5,9},{9,... | collective-permute-start | bytes 147464 | tf_op jit(solution)/shard_map/ppermute | solution.py:18
  13.5 0.0 copy-done.4
  13.5 0.6 neg.4
  14.1 1.2 collective-permute-done.lead_ref
  15.3 0.6 copy-done.15
  16.0 1.6 copy-done.2
  17.5 0.9 copy-done.9
  18.4 0.8 copy-done.11
  19.3 0.8 copy-done.16
  20.1 0.9 copy-done.18
  21.0 36.8 %local_conv.1 = (f32[1024,1024]{1,0:T(8,128)}, f32[16,8,1024]{2,1,0:T(8,128)S(1)}, f32[16,1024]{1,0:T(8,128)S(1)}, bf16[128,1024]{1,0:T(8,128)(2,1)S(1)}) custom-call(bf16[1024,1024]{1,0:T(8,128)(2,1)S(1)} %copy-done.2, bf16[1024,1024]{1,0:T(8,128)(2,1)} %v_ref.1, bf16[3,8,1024]{2,1,0:T(8,128)(2,1)S(1)} %copy-done.16, f32[3,7,1024]{2,1,0:T(8,128)S(1)} %copy-done.9, ...), custom_call_target="tpu_custom_call" | custom-call | tf_op jit(solution)/shard_map/local_conv/pallas_call | solution.py:618
  57.8 0.8 copy-done.5
  58.6 0.7 copy-done.14
  59.3 0.6 copy-done.19
  59.9 29.2 %state_exchange.1 = (f32[8,16,1024]{2,1,0:T(8,128)}, bf16[128,1024]{1,0:T(8,128)(2,1)}) custom-call(f32[16,1024]{1,0:T(8,128)} %copy-done.19, bf16[128,1024]{1,0:T(8,128)(2,1)} %copy-done.14), custom_call_target="tpu_custom_call" | custom-call | tf_op jit(solution)/shard_map/state_exchange/pallas_call | solution.py:225
  89.2 1.2 select_reduce_fusion.start_ref
  90.4 0.0 copy-start.6
  90.4 1.0 copy-done.6
  91.5 0.9 copy-done.10
  92.4 0.9 copy-done.13
  93.3 0.8 copy-done.17
  94.1 13.9 %finish_conv.1.prod_ref = bf16[1024,1024]{1,0:T(8,128)(2,1)S(1)} custom-call(f32[1024,1024]{1,0:T(8,128)} %get-tuple-element.11.y_ref, f32[16,8,1024]{2,1,0:T(8,128)S(1)} %copy-done.6, f32[16,1024]{1,0:T(8,128)S(1)} %select_reduce_fusion.start_ref, bf16[128,1024]{1,0:T(8,128)(2,1)S(1)} %copy-done.13, bf16[1024,1024]{1,0:T(8,128)(2,1)S(1)} %copy-done.1, ...), custom_call_target="tpu_custom_call" | custom-call | tf_op jit(solution)/shard_map/finish_conv/pallas_call | solution.py:647
  108.0 0.0 copy-start
  108.0 1.3 copy-done
  109.3 78.5 %ring_project.1 = bf16[1024,1024]{1,0:T(8,128)(2,1)} custom-call(bf16[1024,1024]{1,0:T(8,128)(2,1)} %copy-done, bf16[1024,2048]{1,0:T(8,128)(2,1)} %all-gather.2.cloned.1.call-done.w_ref, bf16[1024,256]{1,0:T(8,128)(2,1)S(1)} %get-tuple-element.17.own_ref), custom_call_target="tpu_custom_call" | custom-call | tf_op jit(solution)/shard_map/ring_project/pallas_call | solution.py:576
  187.8 3.1 %copy.13 = bf16[1024,1024]{1,0:T(8,128)(2,1)} copy(bf16[1024,1024]{1,0:T(8,128)(2,1)} %ring_project.1) | data formatting | bytes 4194304
  (26 shorter events, 0.1 us)
Async XLA Ops:
  6.5 9.4 %copy-start.7 = (bf16[2,256,128]{2,1,0:T(8,128)(2,1)S(1)}, bf16[2,256,128]{2,1,0:T(8,128)(2,1)}, u32[]{:S(2)}) copy-start(bf16[2,256,128]{2,1,0:T(8,128)(2,1)} %constant.21.clone.fwd_ref) | copy-start | bytes 393220
  6.5 9.4 %copy-start.8 = (bf16[2,128,256]{2,1,0:T(8,128)(2,1)S(1)}, bf16[2,128,256]{2,1,0:T(8,128)(2,1)}, u32[]{:S(2)}) copy-start(bf16[2,128,256]{2,1,0:T(8,128)(2,1)} %constant.23.clone.inv_ref) | copy-start | bytes 393220
  6.5 2.4 %copy-start.1 = (bf16[1024,1024]{1,0:T(8,128)(2,1)S(1)}, bf16[1024,1024]{1,0:T(8,128)(2,1)}, u32[]{:S(2)}) copy-start(bf16[1024,1024]{1,0:T(8,128)(2,1)} %q_ref.1) | copy-start | bytes 6291460
  6.5 6.9 %copy-start.4 = (f32[16,1024]{1,0:T(8,128)S(1)}, f32[16,1024]{1,0:T(8,128)}, u32[]{:S(2)}) copy-start(f32[16,1024]{1,0:T(8,128)} %rate_ref.3) | copy-start | bytes 196612
  6.5 9.4 %copy-start.3 = (f32[128,1024]{1,0:T(8,128)S(1)}, f32[128,1024]{1,0:T(8,128)}, u32[]{:S(2)}) copy-start(f32[128,1024]{1,0:T(8,128)} %taps_ref.3) | copy-start | bytes 1572868
  6.5 102.8 %all-gather.2.cloned.1.call-start = ((), (), s32[]{:S(2)}) async-start(), calls=%async_computation | async-start | bytes 4718592 | tf_op jit(solution)/shard_map/all_gather | solution.py:670
  10.3 5.0 %collective-permute-start = (bf16[3,8,1024]{2,1,0:T(8,128)(2,1)}, bf16[3,8,1024]{2,1,0:T(8,128)(2,1)S(1)}, u32[]{:S(2)}, u32[]{:S(2)}) collective-permute-start(bf16[3,8,1024]{2,1,0:T(8,128)(2,1)} %pad_maximum_fusion), channel_id=1, source_target_pairs={{0,4},{4,8},{8,12},{12,16},{16,20},{20,24},{24,28},{1,5},{5,9},{9,... | collective-permute-start | bytes 147464 | tf_op jit(solution)/shard_map/ppermute | solution.py:18
  15.3 0.6 copy-start.15
  15.9 1.6 copy-start.2
  17.5 0.9 copy-start.9
  18.4 0.8 copy-start.11
  19.3 0.8 copy-start.16
  20.1 0.9 copy-start.18
  21.0 69.4 %copy-start.12 = (f32[16,1024]{1,0:T(8,128)S(1)}, f32[16,1024]{1,0:T(8,128)}, u32[]{:S(2)}) copy-start(f32[16,1024]{1,0:T(8,128)} %res_ref.3) | copy-start | bytes 196612
  57.8 0.8 copy-start.5
  58.6 0.7 copy-start.14
  59.3 0.6 copy-start.19
  90.4 1.1 copy-start.6
  91.5 0.9 copy-start.10
  92.4 0.9 copy-start.13
  93.3 0.8 copy-start.17
  108.0 1.3 copy-start
Sparse Core Ops, SparseCore 0:
  9.4 86.0 all-gather.1

commit v3 on v2

--- a/solution.py
+++ b/solution.py
@@ -103,7 +103,9 @@
             )
         return h_rev + (res_ref[pl.ds(n, 1), :] * jnp.sqrt(2.0 * rate)) * decay
 
-    h_rev = lax.fori_loop(0, modes, one_mode, jnp.zeros((block, LANES), jnp.float32))
+    h_rev = lax.fori_loop(
+        0, modes, one_mode, jnp.zeros((block, LANES), jnp.float32), unroll=2
+    )
 
     step = jnp.exp(-rate_ref[...] * float(block))
     state = ends_ref[:, 0, :]
@@ -390,15 +392,21 @@
         pl.semaphore_signal(barrier, inc=1, device_id={"ctx": peer}, device_id_type=MESH)
     pl.semaphore_wait(barrier, 4)
 
+    hops = peers // 2
+    half = own_ref.shape[0] // 2
+
+    def ring_span(way, hop):
+        return pl.ds(way * half, half) if hop == hops - 1 else pl.ds(0, 2 * half)
+
     def ring_copy(way, hop, first):
         owner = ring_chip(neighbour(-hop if way == 0 else hop), peers)
+        span = ring_span(way, hop)
         return pltpu.make_async_remote_copy(
-            src_ref=own_ref if first else ring.at[owner], dst_ref=ring.at[owner],
+            src_ref=own_ref if first else ring.at[owner, span], dst_ref=ring.at[owner, span],
             send_sem=ring_sems.at[2 * way, hop], recv_sem=ring_sems.at[2 * way + 1, hop],
             device_id={"ctx": behind if way else ahead}, device_id_type=MESH,
         )
 
-    hops = (peers // 2, peers - 1 - peers // 2)
     for way in (0, 1):
         ring_copy(way, 0, True).start()
 
@@ -520,19 +528,6 @@
 
     def arrived(way, hop):
         return ring_chip(neighbour(-hop - 1 if way == 0 else hop + 1), peers)
-
-    for hop in range(hops[0]):
-        ways = [way for way in (0, 1) if hop < hops[way]]
-        for way in ways:
-            pltpu.make_async_remote_copy(
-                src_ref=own_ref, dst_ref=ring.at[arrived(way, hop)],
-                send_sem=ring_sems.at[2 * way, hop], recv_sem=ring_sems.at[2 * way + 1, hop],
-                device_id={"ctx": behind if way else ahead}, device_id_type=MESH,
-            ).wait_recv()
-            if hop + 1 < hops[way]:
-                ring_copy(way, hop + 1, False).start()
-        for way in ways:
-            unit(arrived(way, hop), False)
 
     def finish(t, carry):
         mine_copy(t).wait_recv()
@@ -548,7 +543,22 @@
         mine_copy(t).wait_send()
         return carry
 
-    lax.fori_loop(0, chunks, finish, 0)
+    for hop in range(hops):
+        last = hop == hops - 1
+        if last:
+            lax.fori_loop(0, chunks, finish, 0)
+        for way in (0, 1):
+            span = ring_span(way, hop)
+            pltpu.make_async_remote_copy(
+                src_ref=own_ref.at[span], dst_ref=ring.at[arrived(way, hop), span],
+                send_sem=ring_sems.at[2 * way, hop], recv_sem=ring_sems.at[2 * way + 1, hop],
+                device_id={"ctx": behind if way else ahead}, device_id_type=MESH,
+            ).wait_recv()
+            if not last:
+                ring_copy(way, hop + 1, False).start()
+        for way in (0,) if last else (0, 1):
+            unit(arrived(way, hop), False)
+
     for sub in range(2):
         pair_copy(2 + sub).wait_recv()
         cross_copy(sub).wait_recv()
@@ -560,7 +570,7 @@
         pair_copy(2 + sub).wait_send()
         cross_copy(sub).wait_send()
     for way in (0, 1):
-        for hop in range(hops[way]):
+        for hop in range(hops):
             ring_copy(way, hop, hop == 0).wait_send()
 
 
@@ -614,7 +624,7 @@
     f32, bf16 = jnp.float32, jnp.bfloat16
     lead = shifted(jnp.stack([q_in[-LEAD:], k_in[-LEAD:], v_in[-LEAD:]]), "ctx")
     filt_spec = cols(3, SHORT_LEN)
-    params = pltpu.CompilerParams(vmem_limit_bytes=48 << 20)
+    params = pltpu.CompilerParams(vmem_limit_bytes=62 << 20)
     y_part, ends, state, tail = pl.pallas_call(
         local_kernel,
         grid=grid,

time: 198 us -> 188 us (0.949)
  local copies, waits for them, and re-layouts: 18.9 us -> 7.29 us
    unnamed x41 -> x5, local copies, waits for them, and re-layouts: 15.9 us -> 3.7 us
  transfers between devices with their start and end apart: 2 -> 2, of which waited for: 1 -> 1; matrix products, arithmetic and copies ran while one was open for 2% -> 2% of each run, Pallas kernels for 40% -> 42%
where the time goes in v3:
time: 188 us; the launch traced here: 187 us
  Pallas kernels  159 us (85%)
  between operations  13.5 us (7%)
  local copies, waits for them, and re-layouts  7.29 us (4%)
  starting transfers between devices  3.15 us (2%)
  other arithmetic  1.89 us (1%)
    pallas_call x1, Pallas kernels, ring_project(): pl.pallas_call(functools.partial(ring_project_kernel, peers), in_specs=[v...  79.9 us
    pallas_call x1, Pallas kernels, local(): pl.pallas_call(local_kernel, grid=grid, in_specs=[cols(tokens), cols(toke...  35.2 us
    pallas_call x1, Pallas kernels, exchange(): pl.pallas_call(functools.partial(exchange_kernel, peers), in_specs=[vmem]...  29.8 us
    pallas_call x1, Pallas kernels, local(): pl.pallas_call(finish_kernel, grid=grid, in_specs=[cols(tokens), cols(mod...  14.3 us
  transfers between devices with their start and end apart: 2, of which 1 were waited for; matrix products, arithmetic and copies ran while one was open for 2% of the time, Pallas kernels for 42%

profile of v3, /device:TPU:7, one launch (start us, length us, event | category | flops | bytes accessed | tf_op | source)
XLA Modules:
  0.0 186.6 jit_solution(10631530631974848403)
XLA Ops:
  6.5 0.0 copy-start
  6.5 0.0 all-gather.2.cloned.1.call-start
  6.5 2.1 %fusion.1 = (bf16[1024,256]{1,0:T(8,128)(2,1)S(1)}, bf16[1024,256]{1,0:T(8,128)(2,1)}) fusion(bf16[1024,512]{1,0:T(8,128)(2,1)} %param.18), kind=kLoop, calls=%fused_computation.8 | loop fusion | bytes 2097152 | tf_op jit(solution)/shard_map/slice | solution.py:681
  8.7 0.0 all-gather.2.cloned.1.call-update
  8.7 0.7 slice_bitcast_fusion.2
  9.4 0.7 slice_bitcast_fusion
  10.2 3.1 %collective-permute-start = (bf16[3,8,1024]{2,1,0:T(8,128)(2,1)S(1)}, bf16[3,8,1024]{2,1,0:T(8,128)(2,1)S(1)}, u32[]{:S(2)}, u32[]{:S(2)}) collective-permute-start(bf16[3,8,1024]{2,1,0:T(8,128)(2,1)S(1)} %pad_maximum_fusion), channel_id=1, source_target_pairs={{0,4},{4,8},{8,12},{12,16},{16,20},{20,24},{24,28},{1,5},{5,9},{9,... | collective-permute-start | bytes 147464 | tf_op jit(solution)/shard_map/ppermute | solution.py:18
  13.4 0.0 copy-done
  13.4 1.6 collective-permute-done.lead_ref
  15.0 0.0 copy-start.1
  15.0 0.6 copy-done.1
  15.6 35.2 %local_conv.1 = (f32[1024,1024]{1,0:T(8,128)}, f32[16,8,1024]{2,1,0:T(8,128)}, f32[16,1024]{1,0:T(8,128)}, bf16[128,1024]{1,0:T(8,128)(2,1)}) custom-call(bf16[1024,1024]{1,0:T(8,128)(2,1)} %k_ref.1, bf16[1024,1024]{1,0:T(8,128)(2,1)} %v_ref.1, bf16[3,8,1024]{2,1,0:T(8,128)(2,1)} %copy-done.1, f32[3,7,1024]{2,1,0:T(8,128)} %filt_ref.3, ...), custom_call_target="tpu_custom_call" | custom-call | tf_op jit(solution)/shard_map/local_conv/pallas_call | solution.py:628
  50.9 29.8 %state_exchange.1 = (f32[8,16,1024]{2,1,0:T(8,128)}, bf16[128,1024]{1,0:T(8,128)(2,1)}) custom-call(f32[16,1024]{1,0:T(8,128)} %get-tuple-element.13.state_ref, bf16[128,1024]{1,0:T(8,128)(2,1)} %get-tuple-element.14.tail_ref), custom_call_target="tpu_custom_call" | custom-call | tf_op jit(solution)/shard_map/state_exchange/pallas_call | solution.py:227
  80.7 1.9 select_reduce_fusion.start_ref
  82.5 14.3 %finish_conv.1.prod_ref = bf16[1024,1024]{1,0:T(8,128)(2,1)} custom-call(f32[1024,1024]{1,0:T(8,128)} %get-tuple-element.11.y_ref, f32[16,8,1024]{2,1,0:T(8,128)} %get-tuple-element.12.ends_ref, f32[16,1024]{1,0:T(8,128)} %select_reduce_fusion.start_ref, bf16[128,1024]{1,0:T(8,128)(2,1)} %get-tuple-element.16.tail_ref, bf16[1024,1024]{1,0:T(8,128)(2,1)} %q_ref.1, ...), custom_call_target="tpu_custom_call" | custom-call | tf_op jit(solution)/shard_map/finish_conv/pallas_call | solution.py:657
  96.8 0.0 all-gather.2.cloned.1.call-done.w_ref
  96.8 79.9 %ring_project.1 = bf16[1024,1024]{1,0:T(8,128)(2,1)} custom-call(bf16[1024,1024]{1,0:T(8,128)(2,1)} %finish_conv.1.prod_ref, bf16[1024,2048]{1,0:T(8,128)(2,1)} %all-gather.2.cloned.1.call-done.w_ref, bf16[1024,256]{1,0:T(8,128)(2,1)S(1)} %get-tuple-element.17.own_ref), custom_call_target="tpu_custom_call" | custom-call | tf_op jit(solution)/shard_map/ring_project/pallas_call | solution.py:586
  176.7 3.1 %copy.13 = bf16[1024,1024]{1,0:T(8,128)(2,1)} copy(bf16[1024,1024]{1,0:T(8,128)(2,1)} %ring_project.1) | data formatting | bytes 4194304
  (4 shorter events, 0.0 us)
Async XLA Ops:
  6.5 6.8 %copy-start = (f32[16,1024]{1,0:T(8,128)S(1)}, f32[16,1024]{1,0:T(8,128)}, u32[]{:S(2)}) copy-start(f32[16,1024]{1,0:T(8,128)} %rate_ref.3) | copy-start | bytes 196612
  6.5 90.3 %all-gather.2.cloned.1.call-start = ((), (), s32[]{:S(2)}) async-start(), calls=%async_computation | async-start | bytes 4718592 | tf_op jit(solution)/shard_map/all_gather | solution.py:680
  10.2 4.8 %collective-permute-start = (bf16[3,8,1024]{2,1,0:T(8,128)(2,1)S(1)}, bf16[3,8,1024]{2,1,0:T(8,128)(2,1)S(1)}, u32[]{:S(2)}, u32[]{:S(2)}) collective-permute-start(bf16[3,8,1024]{2,1,0:T(8,128)(2,1)S(1)} %pad_maximum_fusion), channel_id=1, source_target_pairs={{0,4},{4,8},{8,12},{12,16},{16,20},{20,24},{24,28},{1,5},{5,9},{9,... | collective-permute-start | bytes 147464 | tf_op jit(solution)/shard_map/ppermute | solution.py:18
  15.0 0.6 copy-start.1
Sparse Core Ops, SparseCore 0:
  9.4 86.3 all-gather.1

commit v4 on v3

--- a/solution.py
+++ b/solution.py
@@ -78,10 +78,10 @@
 
 
 def local_kernel(
-    k_ref, v_ref, lead_ref, filt_ref, taps_ref, res_ref, rate_ref, fwd_ref, rev_ref, inv_ref,
-    y_ref, ends_ref, state_ref, tail_ref, ks, vs, gs,
+    k_ref, v_ref, lead_ref, filt_ref, res_ref, rate_ref, gated_ref, h_rev_ref, ends_ref,
+    state_ref, tail_ref, ks, vs, gs,
 ):
-    block = taps_ref.shape[0]
+    block = h_rev_ref.shape[0]
     pieces = k_ref.shape[0] // block
     modes = rate_ref.shape[0]
     fill(ks, lead_ref[1], k_ref[...])
@@ -90,7 +90,11 @@
         gated = short_taps(ks, filt_ref[1], b * block, block) * short_taps(
             vs, filt_ref[2], b * block, block
         )
-        gs[b * block : (b + 1) * block] = gated.astype(jnp.bfloat16).astype(jnp.float32)
+        rounded = gated.astype(jnp.bfloat16)
+        gated_ref[b * block : (b + 1) * block] = rounded
+        gs[b * block : (b + 1) * block] = rounded.astype(jnp.float32)
+        if b == pieces - 1:
+            tail_ref[...] = rounded
     rows = lax.broadcasted_iota(jnp.int32, (block, LANES), 0)
     back = (block - 1 - rows).astype(jnp.float32)
 
@@ -103,7 +107,7 @@
             )
         return h_rev + (res_ref[pl.ds(n, 1), :] * jnp.sqrt(2.0 * rate)) * decay
 
-    h_rev = lax.fori_loop(
+    h_rev_ref[...] = lax.fori_loop(
         0, modes, one_mode, jnp.zeros((block, LANES), jnp.float32), unroll=2
     )
 
@@ -113,16 +117,30 @@
         state = step * state + ends_ref[:, b, :]
     state_ref[...] = state
 
+
+def block_kernel(
+    peers, gated_ref, h_rev_ref, taps_ref, fwd_ref, rev_ref, inv_ref, states_ref, tail_ref,
+    y_ref, all_ref, before_ref, landed, landed_tail, send, recv, tail_sems,
+):
+    index = pl.program_id(0)
+
+    @pl.when(index == 0)
+    def _():
+        exchange_start(peers, states_ref, tail_ref, landed, landed_tail, send, recv, tail_sems)
+
+    block = taps_ref.shape[0]
+    pieces = gated_ref.shape[0] // block
+    rows = lax.broadcasted_iota(jnp.int32, (block, LANES), 0)
     row0 = rows == 0
     sign = (1 - 2 * (rows % 2)).astype(jnp.float32)
     sign = jnp.concatenate([sign, sign], 0)
     taps_spec = mm_wide(fwd_ref, taps_ref[...])
-    near_spec = sign * (taps_spec + mm_wide(rev_ref, h_rev))
+    near_spec = sign * (taps_spec + mm_wide(rev_ref, h_rev_ref[...]))
     far = spectrum_parts(taps_spec, block, row0)
     near = spectrum_parts(near_spec, block, row0)
     previous = None
     for b in range(pieces):
-        signal = gs[b * block : (b + 1) * block].astype(jnp.bfloat16)
+        signal = gated_ref[b * block : (b + 1) * block]
         spec = mm(fwd_ref[0], signal) + mm(fwd_ref[1], signal)
         real, imag = spectrum_mul(near, spec, block)
         if previous is not None:
@@ -130,8 +148,12 @@
             real, imag = real + more_real, imag + more_imag
         y_ref[b * block : (b + 1) * block] = mm_wide(inv_ref, jnp.concatenate([real, imag], 0))
         previous = spec
-        if b == pieces - 1:
-            tail_ref[...] = signal
+
+    @pl.when(index == pl.num_programs(0) - 1)
+    def _():
+        exchange_finish(peers, states_ref, tail_ref, landed, landed_tail, send, recv, tail_sems)
+        all_ref[...] = landed[...]
+        before_ref[...] = landed_tail[...]
 
 
 def finish_kernel(
@@ -174,7 +196,21 @@
 MESH = pl.DeviceIdType.MESH
 
 
-def exchange_kernel(peers, state_ref, tail_ref, all_ref, before_ref, send, recv, tail_sems):
+def tail_copy(peer, tail_ref, before_ref, tail_sems):
+    return pltpu.make_async_remote_copy(
+        src_ref=tail_ref, dst_ref=before_ref, send_sem=tail_sems.at[0],
+        recv_sem=tail_sems.at[1], device_id={"ctx": peer}, device_id_type=MESH,
+    )
+
+
+def state_copy(peer, slot, hop, state_ref, all_ref, send, recv):
+    return pltpu.make_async_remote_copy(
+        src_ref=state_ref, dst_ref=all_ref.at[slot], send_sem=send.at[hop],
+        recv_sem=recv.at[slot], device_id={"ctx": peer}, device_id_type=MESH,
+    )
+
+
+def exchange_start(peers, state_ref, tail_ref, all_ref, before_ref, send, recv, tail_sems):
     me = lax.axis_index("ctx")
     barrier = pltpu.get_barrier_semaphore()
     for hop in range(1, peers):
@@ -183,63 +219,33 @@
         )
     pl.semaphore_wait(barrier, peers - 1)
 
-    def tail_copy(peer):
-        return pltpu.make_async_remote_copy(
-            src_ref=tail_ref, dst_ref=before_ref, send_sem=tail_sems.at[0],
-            recv_sem=tail_sems.at[1], device_id={"ctx": peer}, device_id_type=MESH,
-        )
-
-    def state_copy(peer, slot, hop):
-        return pltpu.make_async_remote_copy(
-            src_ref=state_ref, dst_ref=all_ref.at[slot], send_sem=send.at[hop],
-            recv_sem=recv.at[slot], device_id={"ctx": peer}, device_id_type=MESH,
-        )
-
     @pl.when(me < peers - 1)
     def _():
-        tail_copy(me + 1).start()
+        tail_copy(me + 1, tail_ref, before_ref, tail_sems).start()
 
     for hop in range(1, peers):
-        state_copy(lax.rem(me + hop, peers), me, hop).start()
+        state_copy(lax.rem(me + hop, peers), me, hop, state_ref, all_ref, send, recv).start()
     all_ref[me] = state_ref[...]
 
     @pl.when(me == 0)
     def _():
         before_ref[...] = jnp.zeros_like(before_ref)
 
+
+def exchange_finish(peers, state_ref, tail_ref, all_ref, before_ref, send, recv, tail_sems):
+    me = lax.axis_index("ctx")
     for hop in range(1, peers):
         source = lax.rem(me + hop, peers)
-        state_copy(source, source, hop).wait_recv()
-        state_copy(source, me, hop).wait_send()
+        state_copy(source, source, hop, state_ref, all_ref, send, recv).wait_recv()
+        state_copy(source, me, hop, state_ref, all_ref, send, recv).wait_send()
 
     @pl.when(me > 0)
     def _():
-        tail_copy(me).wait_recv()
+        tail_copy(me, tail_ref, before_ref, tail_sems).wait_recv()
 
     @pl.when(me < peers - 1)
     def _():
-        tail_copy(me + 1).wait_send()
-
-
-def exchange(state, tail):
-    peers = lax.axis_size("ctx")
-    vmem = pl.BlockSpec(memory_space=pltpu.VMEM)
-    return pl.pallas_call(
-        functools.partial(exchange_kernel, peers),
-        in_specs=[vmem] * 2,
-        out_specs=[vmem] * 2,
-        out_shape=[
-            jax.ShapeDtypeStruct((peers,) + state.shape, state.dtype),
-            jax.ShapeDtypeStruct(tail.shape, tail.dtype),
-        ],
-        scratch_shapes=[
-            pltpu.SemaphoreType.DMA((peers,)),
-            pltpu.SemaphoreType.DMA((peers,)),
-            pltpu.SemaphoreType.DMA((2,)),
-        ],
-        compiler_params=pltpu.CompilerParams(collective_id=0, has_side_effects=True),
-        name="state_exchange",
-    )(state, tail)
+        tail_copy(me + 1, tail_ref, before_ref, tail_sems).wait_send()
 
 
 def project_kernel(
@@ -625,16 +631,16 @@
     lead = shifted(jnp.stack([q_in[-LEAD:], k_in[-LEAD:], v_in[-LEAD:]]), "ctx")
     filt_spec = cols(3, SHORT_LEN)
     params = pltpu.CompilerParams(vmem_limit_bytes=62 << 20)
-    y_part, ends, state, tail = pl.pallas_call(
+    gated, h_rev, ends, state, tail = pl.pallas_call(
         local_kernel,
         grid=grid,
         in_specs=[
-            cols(tokens), cols(tokens), cols(3, LEAD), filt_spec, cols(block), cols(modes),
-            cols(modes), whole(fwd.shape), whole(rev.shape), whole(inv.shape),
-        ],
-        out_specs=[cols(tokens), cols(modes, pieces), cols(modes), cols(block)],
+            cols(tokens), cols(tokens), cols(3, LEAD), filt_spec, cols(modes), cols(modes),
+        ],
+        out_specs=[cols(tokens), cols(block), cols(modes, pieces), cols(modes), cols(block)],
         out_shape=[
-            jax.ShapeDtypeStruct((tokens, chans), f32),
+            jax.ShapeDtypeStruct((tokens, chans), bf16),
+            jax.ShapeDtypeStruct((block, chans), f32),
             jax.ShapeDtypeStruct((modes, pieces, chans), f32),
             jax.ShapeDtypeStruct((modes, chans), f32),
             jax.ShapeDtypeStruct((block, chans), bf16),
@@ -645,10 +651,36 @@
             pltpu.VMEM((tokens, LANES), f32),
         ],
         compiler_params=params,
-        name="local_conv",
-    )(k_in, v_in, lead, short_filter, taps, residue, rate, fwd, rev, inv)
-
-    all_states, before = exchange(state, tail)
+        name="gate",
+    )(k_in, v_in, lead, short_filter, residue, rate)
+
+    peers = lax.axis_size("ctx")
+    all_shape = (peers,) + state.shape
+    y_part, all_states, before = pl.pallas_call(
+        functools.partial(block_kernel, peers),
+        grid=grid,
+        in_specs=[
+            cols(tokens), cols(block), cols(block), whole(fwd.shape), whole(rev.shape),
+            whole(inv.shape), whole(state.shape), whole(tail.shape),
+        ],
+        out_specs=[cols(tokens), whole(all_shape), whole(tail.shape)],
+        out_shape=[
+            jax.ShapeDtypeStruct((tokens, chans), f32),
+            jax.ShapeDtypeStruct(all_shape, f32),
+            jax.ShapeDtypeStruct(tail.shape, bf16),
+        ],
+        scratch_shapes=[
+            pltpu.VMEM(all_shape, f32),
+            pltpu.VMEM(tail.shape, bf16),
+            pltpu.SemaphoreType.DMA((peers,)),
+            pltpu.SemaphoreType.DMA((peers,)),
+            pltpu.SemaphoreType.DMA((2,)),
+        ],
+        compiler_params=pltpu.CompilerParams(
+            collective_id=0, has_side_effects=True, vmem_limit_bytes=62 << 20
+        ),
+        name="block_conv",
+    )(gated, h_rev, taps, fwd, rev, inv, state, tail)
     gap = lax.axis_index("ctx") - 1 - jnp.arange(all_states.shape[0])
     spans = (jnp.maximum(gap, 0) * tokens).astype(f32)[:, None, None]
     carried = jnp.where((gap >= 0)[:, None, None], jnp.exp(-rate[None] * spans) * all_states, 0.0)

time: 188 us -> 169 us (0.90)
  Pallas kernels: 159 us -> 121 us
  waiting for transfers between devices: 1.65 us -> 22.1 us
    all_gather x1, waiting for transfers between devices: 0.02 us -> 20.5 us  [local(): early = lax.all_gather(out_weight[:, :half], 'ctx', axis=1, tiled=True)]
    pallas_call x1, Pallas kernels: 35.2 us -> 14.8 us  [local(): pl.pallas_call(local_kernel, grid=grid, in_specs=[cols(tokens), cols(toke...]
    pallas_call x1, Pallas kernels: 79.9 us -> 64.2 us  [ring_project(): pl.pallas_call(functools.partial(ring_project_kernel, peers), in_specs=[v...]
    pallas_call x1, Pallas kernels: 29.8 us -> 27.7 us  [local(): pl.pallas_call(functools.partial(block_kernel, peers), grid=grid, in_spec...]
  transfers between devices with their start and end apart: 2 -> 2, of which waited for: 1 -> 2; matrix products, arithmetic and copies ran while one was open for 2% -> 2% of each run, Pallas kernels for 42% -> 34%
where the time goes in v4:
time: 169 us
  Pallas kernels  121 us (72%)
  waiting for transfers between devices  22.1 us (13%)
  between operations  13.5 us (8%)
  local copies, waits for them, and re-layouts  7.29 us (4%)
  starting transfers between devices  3.15 us (2%)
  other arithmetic  1.89 us (1%)
    pallas_call x1, Pallas kernels, ring_project(): pl.pallas_call(functools.partial(ring_project_kernel, peers), in_specs=[v...  64.2 us
    pallas_call x1, Pallas kernels, local(): pl.pallas_call(functools.partial(block_kernel, peers), grid=grid, in_spec...  27.7 us
    all_gather x1, waiting for transfers between devices, local(): early = lax.all_gather(out_weight[:, :half], 'ctx', axis=1, tiled=True)  20.5 us
    pallas_call x1, Pallas kernels, local(): pl.pallas_call(local_kernel, grid=grid, in_specs=[cols(tokens), cols(toke...  14.8 us
    pallas_call x1, Pallas kernels, local(): pl.pallas_call(finish_kernel, grid=grid, in_specs=[cols(tokens), cols(mod...  14.2 us
    unnamed x5, local copies, waits for them, and re-layouts  3.7 us
  transfers between devices with their start and end apart: 2, of which 2 were waited for; matrix products, arithmetic and copies ran while one was open for 2% of the time, Pallas kernels for 34%

profile of v4, /device:TPU:7, one launch (start us, length us, event | category | flops | bytes accessed | tf_op | source)
XLA Modules:
  0.0 168.8 jit_solution(10684407793594866106)
XLA Ops:
  6.5 0.0 copy-start
  6.5 0.0 all-gather.2.cloned.1.call-start
  6.5 2.1 %fusion.1 = (bf16[1024,256]{1,0:T(8,128)(2,1)S(1)}, bf16[1024,256]{1,0:T(8,128)(2,1)}) fusion(bf16[1024,512]{1,0:T(8,128)(2,1)} %param.18), kind=kLoop, calls=%fused_computation.8 | loop fusion | bytes 2097152 | tf_op jit(solution)/shard_map/slice | solution.py:713
  8.7 0.0 all-gather.2.cloned.1.call-update
  8.7 0.7 slice_bitcast_fusion.2
  9.4 0.7 slice_bitcast_fusion
  10.2 3.1 %collective-permute-start = (bf16[3,8,1024]{2,1,0:T(8,128)(2,1)S(1)}, bf16[3,8,1024]{2,1,0:T(8,128)(2,1)S(1)}, u32[]{:S(2)}, u32[]{:S(2)}) collective-permute-start(bf16[3,8,1024]{2,1,0:T(8,128)(2,1)S(1)} %pad_maximum_fusion), channel_id=1, source_target_pairs={{0,4},{4,8},{8,12},{12,16},{16,20},{20,24},{24,28},{1,5},{5,9},{9,... | collective-permute-start | bytes 147464 | tf_op jit(solution)/shard_map/ppermute | solution.py:18
  13.4 0.0 copy-done
  13.4 1.6 collective-permute-done.lead_ref
  15.0 0.0 copy-start.1
  15.0 0.6 copy-done.1
  15.6 14.8 %gate.1 = (bf16[1024,1024]{1,0:T(8,128)(2,1)}, f32[128,1024]{1,0:T(8,128)}, f32[16,8,1024]{2,1,0:T(8,128)}, f32[16,1024]{1,0:T(8,128)}, bf16[128,1024]{1,0:T(8,128)(2,1)}) custom-call(bf16[1024,1024]{1,0:T(8,128)(2,1)} %k_ref.1, bf16[1024,1024]{1,0:T(8,128)(2,1)} %v_ref.1, bf16[3,8,1024]{2,1,0:T(8,128)(2,1)} %copy-done.1, f32[3,7,1024]{2,1,0:T(8,128)} %filt_ref.3, ...), custom_call_target="tpu_custom_call" | custom-call | tf_op jit(solution)/shard_map/gate/pallas_call | solution.py:634
  30.4 27.7 %block_conv.1 = (f32[1024,1024]{1,0:T(8,128)}, f32[8,16,1024]{2,1,0:T(8,128)}, bf16[128,1024]{1,0:T(8,128)(2,1)}) custom-call(bf16[1024,1024]{1,0:T(8,128)(2,1)} %get-tuple-element.13.gated_ref, f32[128,1024]{1,0:T(8,128)} %get-tuple-element.14.h_rev_ref, f32[128,1024]{1,0:T(8,128)} %taps_ref.3, bf16[2,256,128]{2,1,0:T(8,128)(2,1)} %constant.21.clone.fwd_ref, ...), custom_call_target="tpu_custom_call" | custom-call | tf_op jit(solution)/shard_map/block_conv/pallas_call | solution.py:659
  58.1 1.9 %select_reduce_fusion.start_ref = f32[16,1024]{1,0:T(8,128)} fusion(f32[8,16,1024]{2,1,0:T(8,128)} %get-tuple-element.19, f32[8]{0:T(128)S(1)} %multiply_convert_fusion, f32[16,1024]{1,0:T(8,128)S(1)} %neg.4, pred[8]{0:T(512)(128)(4,1)S(1)} %fusion), kind=kLoop, calls=%fused_computation | loop fusion | flops 507904 | bytes 655400 | tf_op jit(solution)/shard_map/reduce_sum | solution.py:687
  60.0 14.2 %finish_conv.1.prod_ref = bf16[1024,1024]{1,0:T(8,128)(2,1)} custom-call(f32[1024,1024]{1,0:T(8,128)} %get-tuple-element.17.y_ref, f32[16,8,1024]{2,1,0:T(8,128)} %get-tuple-element.18.ends_ref, f32[16,1024]{1,0:T(8,128)} %select_reduce_fusion.start_ref, bf16[128,1024]{1,0:T(8,128)(2,1)} %get-tuple-element.20.tail_ref, bf16[1024,1024]{1,0:T(8,128)(2,1)} %q_ref.1, ...), custom_call_target="tpu_custom_call" | custom-call | tf_op jit(solution)/shard_map/finish_conv/pallas_call | solution.py:689
  74.2 20.5 %all-gather.2.cloned.1.call-done.w_ref = bf16[1024,2048]{1,0:T(8,128)(2,1)} async-done(((bf16[1024,256]{1,0:T(8,128)(2,1)}), bf16[1024,2048]{1,0:T(8,128)(2,1)}) %all-gather.2.cloned.1.call-update) | async-done | bytes 4194320 | tf_op jit(solution)/shard_map/all_gather | solution.py:712
  94.7 64.2 %ring_project.1 = bf16[1024,1024]{1,0:T(8,128)(2,1)} custom-call(bf16[1024,1024]{1,0:T(8,128)(2,1)} %finish_conv.1.prod_ref, bf16[1024,2048]{1,0:T(8,128)(2,1)} %all-gather.2.cloned.1.call-done.w_ref, bf16[1024,256]{1,0:T(8,128)(2,1)S(1)} %get-tuple-element.21.own_ref), custom_call_target="tpu_custom_call" | custom-call | tf_op jit(solution)/shard_map/ring_project/pallas_call | solution.py:592
  158.9 3.1 %copy.13 = bf16[1024,1024]{1,0:T(8,128)(2,1)} copy(bf16[1024,1024]{1,0:T(8,128)(2,1)} %ring_project.1) | data formatting | bytes 4194304
  (4 shorter events, 0.0 us)
Async XLA Ops:
  6.5 6.8 %copy-start = (f32[16,1024]{1,0:T(8,128)S(1)}, f32[16,1024]{1,0:T(8,128)}, u32[]{:S(2)}) copy-start(f32[16,1024]{1,0:T(8,128)} %rate_ref.3) | copy-start | bytes 196612
  6.5 88.2 %all-gather.2.cloned.1.call-start = ((), (), s32[]{:S(2)}) async-start(), calls=%async_computation | async-start | bytes 4718592 | tf_op jit(solution)/shard_map/all_gather | solution.py:712
  10.2 4.8 %collective-permute-start = (bf16[3,8,1024]{2,1,0:T(8,128)(2,1)S(1)}, bf16[3,8,1024]{2,1,0:T(8,128)(2,1)S(1)}, u32[]{:S(2)}, u32[]{:S(2)}) collective-permute-start(bf16[3,8,1024]{2,1,0:T(8,128)(2,1)S(1)} %pad_maximum_fusion), channel_id=1, source_target_pairs={{0,4},{4,8},{8,12},{12,16},{16,20},{20,24},{24,28},{1,5},{5,9},{9,... | collective-permute-start | bytes 147464 | tf_op jit(solution)/shard_map/ppermute | solution.py:18
  15.0 0.6 copy-start.1
Sparse Core Ops, SparseCore 0:
  9.4 85.2 all-gather.1
